TPU v7x, 32 devices: a whole 2x2x4 slice. The times are simulated.
32 devices in a mesh: dom: 8 (over y, x, core), rep: 4 (over z).
Axes of the slice: x: 2, y: 2, z: 4, core: 2. Of those that a mesh axis runs over, the one named last changes fastest.
Arguments:
- hop_feats: bfloat16 [3, 65536, 128], P(None, ('dom', 'rep')), may hold values from -6 to 6
- adj_local: bfloat16 [512, 12, 128, 128], P(('dom', 'rep')), may hold values from -0.125 to 0.125
- local_cols: int32 [512, 12], P(('dom', 'rep')), may hold values from 0 to 15
- adj_halo: bfloat16 [512, 4, 128, 128], P(('dom', 'rep')), may hold values from -0.125 to 0.125
- halo_cols: int32 [512, 4], P(('dom', 'rep')), may hold values from 0 to 3
- boundary_rows: int32 [32, 512], P(('dom', 'rep')), may hold values from 0 to 2047
- train_ids: int32 [32, 2048], P(('dom', 'rep')), may hold values from 0 to 2047, as said below
- shuffle: int32 [32, 2048], P(('dom', 'rep')), may hold values from 0 to 2047, as said below
- labels: int32 [65536], P(('dom', 'rep')), may hold values from 0 to 171
- labelled: int32 [65536], P(('dom', 'rep')), may hold values from 0 to 1
- w_first: bfloat16 [512, 1024], P(None, 'rep'), may hold values from -1 to 1
- w_second: bfloat16 [1024, 172], P('rep'), may hold values from -2 to 2
Outputs:
- next_hop: bfloat16 [65536, 128], P(('dom', 'rep'))
- batch_loss: float32 [32, 32], P(('dom', 'rep'))
- grad_first: float32 [512, 1024], P('dom', 'rep')
- grad_second: float32 [1024, 172], P('rep')
Inputs may be any that keep to these rules, and one draw needn't show every extreme that they name: `local_cols`: local tile indices of the partition's own row tiles. `halo_cols`: indices of received boundary tiles. `boundary_rows`: rows of the sending partition itself. `train_ids`: rows of the partition itself. `shuffle`: each row is a permutation of 0 .. 2047.
All inputs are finite; a program needn't handle non-finite values.
Results may differ from a plain program's by a relative error of at most 0.005.
The roundings to bfloat16 on the way count: a program that leaves them out, or rounds other values in their place, can miss the bound.
Values may be sent and summed in bfloat16 or wider, within the bound.
No kernel may reach another device: no remote copies, remote signals or barrier semaphores. Data moves between devices by JAX's collectives and lax.ppermute only.
A program may use at most 128 MiB of HBM per device.

v0:
```python
import jax
import jax.numpy as jnp
from jax import lax
from jax.sharding import PartitionSpec as P


def loss_head(logits, targets, weights_row):
    row_max = jnp.max(logits, axis=1, keepdims=True)
    expos = jnp.exp(logits - row_max)
    totals = jnp.sum(expos, axis=1, keepdims=True)
    classes = lax.broadcasted_iota(jnp.int32, logits.shape, 1)
    onehot = (classes == targets[:, None]).astype(jnp.float32)
    cross = jnp.log(totals[:, 0]) + row_max[:, 0] - jnp.sum(onehot * logits, axis=1)
    count = jnp.maximum(jnp.sum(weights_row), 1.0)
    dlogits = ((expos / totals - onehot) * (weights_row / count)[:, None]).astype(jnp.bfloat16)
    return (cross, dlogits)


def source_losses(cross, weights_row, groups):
    masks = weights_row.reshape(groups, -1)
    sums = jnp.sum(masks * cross.reshape(groups, -1), axis=1)
    return sums / jnp.maximum(jnp.sum(masks, axis=1), 1.0)


def batch_norm(pre):
    center = pre - jnp.mean(pre, axis=-2, keepdims=True)
    rstd = lax.rsqrt(jnp.mean(center * center, axis=-2, keepdims=True) + 1e-05)
    return (center * rstd, rstd)


def norm_back(grad, normed, rstd):
    mean_grad = jnp.mean(grad, axis=-2, keepdims=True)
    mean_proj = jnp.mean(grad * normed, axis=-2, keepdims=True)
    return (grad - mean_grad - normed * mean_proj) * rstd


def contract_rows(left, right):
    return lax.dot_general(
        left, right, (((0,), (0,)), ((), ())), preferred_element_type=jnp.float32
    )


def shards(
    hop_feats,
    adj_local,
    local_cols,
    adj_halo,
    halo_cols,
    boundary_rows,
    train_ids,
    shuffle,
    labels,
    labelled,
    w_first,
    w_second,
):
    num_dom = lax.axis_size("dom")
    num_rep = lax.axis_size("rep")
    devices = num_dom * num_rep
    tile = adj_local.shape[-1]
    row_tiles = adj_local.shape[0]
    rows = row_tiles * tile
    width = hop_feats.shape[2]
    hop_two = hop_feats[2]
    sent = jnp.take(hop_two, boundary_rows[0], axis=0)
    halo = lax.all_to_all(sent, ("dom", "rep"), split_axis=0, concat_axis=0, tiled=True)
    halo_count = halo.shape[0] // tile
    own_tiles = hop_two.reshape(row_tiles, tile, width)
    near = jnp.take(own_tiles, local_cols, axis=0)
    summed = jnp.einsum("ikab,ikbc->iac", adj_local, near, preferred_element_type=jnp.float32)
    far = jnp.take(halo.reshape(halo_count, tile, width), halo_cols, axis=0)
    summed = summed + jnp.einsum(
        "ikab,ikbc->iac", adj_halo, far, preferred_element_type=jnp.float32
    )
    next_hop = summed.reshape(rows, width).astype(jnp.bfloat16)
    order = jnp.take(train_ids[0], shuffle[0], axis=0)
    allfeat = jnp.concatenate([hop_feats[0], hop_feats[1], hop_two, next_hop], axis=1)
    feats = jnp.take(allfeat, order, axis=0)
    own_labels = jnp.take(labels, order, axis=0)
    own_marks = jnp.take(labelled, order, axis=0)
    target_pair = jnp.stack([own_labels, own_marks], axis=0)
    batch = lax.all_to_all(feats, ("dom", "rep"), split_axis=0, concat_axis=0, tiled=True)
    got_pair = lax.all_to_all(target_pair, ("dom", "rep"), split_axis=1, concat_axis=1, tiled=True)
    targets = got_pair[0]
    weights_row = got_pair[1].astype(jnp.float32)
    first_whole, second_whole = (
        lax.all_gather(w_first, "rep", axis=1, tiled=True),
        lax.all_gather(w_second, "rep", axis=0, tiled=True),
    )
    hidden_pre = jnp.dot(batch, first_whole, preferred_element_type=jnp.float32)
    normed, rstd = batch_norm(hidden_pre)
    hidden = jnp.maximum(normed, 0.0).astype(jnp.bfloat16)
    logits = jnp.dot(hidden, second_whole, preferred_element_type=jnp.float32)
    cross, dlogits = loss_head(logits, targets, weights_row)
    grad_two_full = contract_rows(hidden, dlogits)
    dhidden = lax.dot_general(
        dlogits, second_whole, (((1,), (1,)), ((), ())), preferred_element_type=jnp.float32
    )
    masked = jnp.where(normed > 0, dhidden, 0.0)
    dpre = norm_back(masked, normed, rstd).astype(jnp.bfloat16)
    grad_one_full = contract_rows(batch, dpre)
    grad_one_rep, grad_two_rep = (
        lax.psum_scatter(grad_one_full, "rep", scatter_dimension=1, tiled=True),
        lax.psum_scatter(grad_two_full, "rep", scatter_dimension=0, tiled=True),
    )
    grad_one = lax.psum_scatter(grad_one_rep, "dom", scatter_dimension=0, tiled=True)
    grad_two = lax.psum(grad_two_rep, "dom")
    loss = source_losses(cross, weights_row, devices)
    return (next_hop, loss.reshape(1, devices), grad_one, grad_two)


def solution(mesh):
    placed = (
        P(None, ("dom", "rep"), None),
        P(("dom", "rep"), None, None, None),
        P(("dom", "rep"), None),
        P(("dom", "rep"), None, None, None),
        P(("dom", "rep"), None),
        P(("dom", "rep"), None),
        P(("dom", "rep"), None),
        P(("dom", "rep"), None),
        P(("dom", "rep")),
        P(("dom", "rep")),
        P(None, "rep"),
        P("rep", None),
    )
    return jax.shard_map(
        shards,
        mesh=mesh,
        in_specs=placed,
        out_specs=(
            P(("dom", "rep"), None),
            P(("dom", "rep"), None),
            P("dom", "rep"),
            P("rep", None),
        ),
        check_vma=False,
    )
```

profile of v0, /device:TPU:0, one launch (start us, length us, event | category | flops | bytes accessed | tf_op | source)
XLA Modules:
  0.0 375.0 jit_solution(16362593156664925678)
XLA Ops:
  7.2 0.8 compare_select_fusion.5
  8.0 0.5 broadcast.147
  8.5 1.3 reduce.13
  10.0 2.6 slice_bitcast_fusion.1
  12.7 1.3 gather_fusion.1
  14.0 0.8 broadcast_select_fusion.1
  14.8 7.3 %all-to-all-start = ((bf16[32,16,128]{2,1,0:T(8,128)(2,1)}), bf16[32,16,128]{2,1,0:T(8,128)(2,1)S(1)}, u32[]{:S(2)}, u32[]{:S(2)}) async-start(bf16[32,16,128]{2,1,0:T(8,128)(2,1)} %broadcast_select_fusion.1), calls=%async_computation | async-start | bytes 262144 | tf_op jit(solution)/shard_map/all_to_all | solution.py:66
  22.4 11.8 %gather_fusion.4 = s32[2048]{0:T(1024)S(1)} fusion(s32[2048]{0:T(1024)S(1)} %bitcast.44, s32[2048]{0:T(1024)S(1)} %fusion.25), kind=kCustom, calls=%fused_computation.clone | custom fusion | bytes 24576 | tf_op jit(solution)/shard_map/jit(_take)/gather | solution.py:76
  34.2 0.7 copy-done.2
  34.9 11.8 %gather_fusion.6 = s32[2048]{0:T(1024)S(1)} fusion(s32[2048]{0:T(1024)S(1)} %copy-done.2, s32[2048]{0:T(1024)S(1)} %broadcast_clamp_fusion), kind=kCustom, calls=%fused_computation.2.clone | custom fusion | bytes 24576 | tf_op jit(solution)/shard_map/jit(_take)/gather | solution.py:80
  46.7 11.8 %gather_fusion.5 = s32[2048]{0:T(1024)S(1)} fusion(s32[2048]{0:T(1024)S(1)} %copy-done.3, s32[2048]{0:T(1024)S(1)} %broadcast_clamp_fusion), kind=kCustom, calls=%fused_computation.1.clone | custom fusion | bytes 24576 | tf_op jit(solution)/shard_map/jit(_take)/gather | solution.py:79
  59.0 0.7 reshape.253
  59.7 8.0 %gather_fusion = bf16[192,128,128]{2,1,0:T(8,128)(2,1)} fusion(bf16[16,128,128]{2,1,0:T(8,128)(2,1)S(1)} %bitcast.45, s32[1024]{0:T(1024)S(1)} %pad_clamp_fusion.2), kind=kCustom, calls=%fused_computation.3 | custom fusion | bytes 12583680 | tf_op jit(solution)/shard_map/jit(_take)/gather | solution.py:69
  67.7 5.8 %all-to-all-start.1 = ((s32[32,1,128]{2,1,0:T(1,128)}), s32[32,1,128]{2,1,0:T(1,128)S(1)}, u32[]{:S(2)}, u32[]{:S(2)}) async-start(s32[32,1,128]{2,1,0:T(1,128)} %reshape.253), calls=%async_computation.1 | async-start | bytes 32768 | tf_op jit(solution)/shard_map/all_to_all | solution.py:83
  73.6 2.2 gather_fusion.2
  75.8 2.4 fusion.9
  78.1 6.6 %fusion.18 = bf16[16,128,128]{1,2,0:T(8,128)(2,1)S(1)} fusion(f32[16,128,128]{1,2,0:T(8,128)S(1)} %fusion.9, bf16[16,12,128,128]{3,2,1,0:T(8,128)(2,1)} %param.15, bf16[16,12,128,128]{3,2,1,0:T(8,128)(2,1)} %bitcast.48, pred[16,12]{1,0:T(8,128)(4,1)S(1)} %compare_and_fusion.2), kind=kOutput, calls=%fused_computation.31 | convolution fusion | flops 808976384 | bytes 14155968 | tf_op jit(solution)/shard_map/ikab,ikbc->iac/dot_general | solution.py:70
  84.7 0.8 copy-done.8
  85.5 1.6 pad_maximum_fusion
  87.1 11.1 %gather_fusion.3 = bf16[2048,512]{1,0:T(8,128)(2,1)} fusion(bf16[2048,512]{1,0:T(8,128)(2,1)} %pad_maximum_fusion, s32[2048]{0:T(1024)S(1)} %broadcast_clamp_fusion), kind=kCustom, calls=%fused_computation.6 | custom fusion | bytes 4202496 | tf_op jit(solution)/shard_map/jit(_take)/gather | solution.py:78
  98.2 2.8 broadcast_select_fusion
  101.0 6.0 %all-to-all-start.2 = ((bf16[32,64,512]{2,1,0:T(8,128)(2,1)}), bf16[32,64,512]{2,1,0:T(8,128)(2,1)}, u32[]{:S(2)}, u32[]{:S(2)}) async-start(bf16[32,64,512]{2,1,0:T(8,128)(2,1)} %broadcast_select_fusion), calls=%async_computation.2 | async-start | bytes 4194304 | tf_op jit(solution)/shard_map/all_to_all | solution.py:82
  107.0 0.7 all-gather.2.cloned.1.call-update
  107.7 73.9 %all_gather.7 = bf16[1024,172]{0,1:T(8,128)(2,1)} all-gather(bf16[256,172]{0,1:T(8,128)(2,1)S(1)} %copy-done.9), channel_id=1, replica_groups=mesh['dom'=8,'rep'=4] {'rep'}, dimensions={0}, use_global_device_ids=true | all-gather | bytes 440320 | tf_op jit(solution)/shard_map/all_gather | solution.py:88
  181.7 0.5 broadcast.150
  182.2 0.7 reduce.14
  183.0 0.6 fusion.32
  184.3 0.8 divide_reduce_fusion
  185.1 0.7 div.54
  185.8 0.6 slice_reduce_fusion
  186.4 0.7 eq.10
  187.1 4.2 %fusion.35 = (f32[1024]{0:T(1024)S(1)}, f32[2048,1024]{1,0:T(8,128)S(1)}) fusion(bf16[2048,512]{1,0:T(8,128)(2,1)} %bitcast.21, bf16[512,1024]{1,0:T(8,128)(2,1)} %all-gather.2.cloned.1.call-done), kind=kOutput, calls=%fused_computation.77 | convolution fusion | flops 2149579776 | bytes 11538432 | tf_op jit(solution)/shard_map/dot_general | solution.py:90
  191.3 0.9 multiply_reduce_fusion.1
  192.2 0.3 copy-done.7
  192.6 1.6 fusion.36
  194.2 1.0 fusion.21
  195.2 0.6 copy-done.13
  195.8 2.5 fusion.23
  198.3 7.4 %fusion = (f32[1024]{0:T(1024)}, f32[1024]{0:T(1024)}, f32[2048,1024]{1,0:T(8,128)}) fusion(f32[2048,1024]{1,0:T(8,128)} %copy-done.4, f32[1024]{0:T(1024)S(1)} %add_rsqrt_fusion, f32[1024]{0:T(1024)S(1)} %broadcast_multiply_fusion.2, bf16[1024,172]{0,1:T(8,128)(2,1)} %all_gather.7, f32[2048,172]{0,1:T(8,128)S(1)} %get-tuple-element.22, f32[2048]{0:T(1024)} %div.54, ...), kind=kOutput, calls=%fused_computation.13 | convolution fusion | flops 738564096 | bytes 18587648 | tf_op jit(solution)/shard_map/dot_general | solution.py:96
  205.8 0.7 broadcast_multiply_fusion
  206.5 10.6 %fusion.4 = f32[512,1024]{1,0:T(8,128)} fusion(bf16[2048,512]{1,0:T(8,128)(2,1)} %bitcast.21, f32[2048,1024]{1,0:T(8,128)} %get-tuple-element.23, f32[2048,1024]{1,0:T(8,128)} %copy-done.4, f32[1024]{0:T(1024)S(1)} %get-tuple-element.24, f32[1024]{0:T(1024)S(1)} %get-tuple-element.25, f32[1024]{0:T(1024)S(1)} %add_rsqrt_fusion, ...), kind=kOutput, calls=%fused_computation.17 | convolution fusion | flops 2166358016 | bytes 20987904 | tf_op jit(solution)/shard_map/dot_general | solution.py:38
  217.2 11.8 %reduce-scatter.8.cloned.1.call-done = f32[256,172]{0,1:T(8,128)} async-done(((f32[1024,172]{0,1:T(8,128)}), f32[256,172]{0,1:T(8,128)}) %reduce-scatter.8.cloned.1.call-update) | async-done | bytes 176144 | tf_op jit(solution)/shard_map/reduce_scatter | solution.py:104
  229.0 44.9 %reduce-scatter.4.cloned.1.call-done = f32[512,256]{1,0:T(8,128)} async-done(((f32[512,1024]{1,0:T(8,128)}), f32[512,256]{1,0:T(8,128)}) %reduce-scatter.4.cloned.1.call-update) | async-done | bytes 524304 | tf_op jit(solution)/shard_map/reduce_scatter | solution.py:103
  274.0 0.1 multiply_reduce_fusion.2
  274.2 0.5 fusion.26
  274.7 54.4 %all-reduce.2.cloned.1.call-done = f32[256,172]{0,1:T(8,128)} async-done(((f32[256,172]{0,1:T(8,128)}), f32[256,172]{0,1:T(8,128)}) %all-reduce.2.cloned.1.call-update) | async-done | bytes 176144 | tf_op jit(solution)/shard_map/psum | solution.py:107
  329.1 37.7 %reduce-scatter.6.cloned.1.call-done = f32[64,256]{1,0:T(8,128)} async-done(((f32[512,256]{1,0:T(8,128)}), f32[64,256]{1,0:T(8,128)}) %reduce-scatter.6.cloned.1.call-update) | async-done | bytes 65552 | tf_op jit(solution)/shard_map/reduce_scatter | solution.py:106
  366.9 1.6 copy.25
  (75 shorter events, 1.3 us)
Async XLA Ops:
  7.2 68.6 %copy-start = (bf16[16,4,128,128]{3,2,1,0:T(8,128)(2,1)S(1)}, bf16[16,4,128,128]{3,2,1,0:T(8,128)(2,1)}, u32[]{:S(2)}) copy-start(bf16[16,4,128,128]{3,2,1,0:T(8,128)(2,1)} %param.17) | copy-start | bytes 6291460
  10.0 12.1 %copy-start.18 = (s32[16,4]{0,1:T(4,128)S(1)}, s32[16,4]{0,1:T(4,128)}, u32[]{:S(2)}) copy-start(s32[16,4]{0,1:T(4,128)} %param.18) | copy-start | bytes 772
  10.0 12.4 %copy-start.10 = (s32[1,2048]{1,0:T(1,128)S(1)}, s32[1,2048]{1,0:T(1,128)}, u32[]{:S(2)}) copy-start(s32[1,2048]{1,0:T(1,128)} %param.21) | copy-start | bytes 24580
  10.0 12.4 %copy-start.1 = (s32[1,2048]{1,0:T(1,128)S(1)}, s32[1,2048]{1,0:T(1,128)}, u32[]{:S(2)}) copy-start(s32[1,2048]{1,0:T(1,128)} %param.20) | copy-start | bytes 24580
  14.8 53.0 %all-to-all-start = ((bf16[32,16,128]{2,1,0:T(8,128)(2,1)}), bf16[32,16,128]{2,1,0:T(8,128)(2,1)S(1)}, u32[]{:S(2)}, u32[]{:S(2)}) async-start(bf16[32,16,128]{2,1,0:T(8,128)(2,1)} %broadcast_select_fusion.1), calls=%async_computation | async-start | bytes 262144 | tf_op jit(solution)/shard_map/all_to_all | solution.py:66
  34.2 0.7 copy-start.2
  34.9 11.8 %copy-start.3 = (s32[2048]{0:T(1024)S(1)}, s32[2048]{0:T(1024)}, u32[]{:S(2)}) copy-start(s32[2048]{0:T(1024)} %param.22) | copy-start | bytes 24580
  46.7 12.0 %copy-start.16 = (s32[16,12]{1,0:T(8,128)S(1)}, s32[16,12]{1,0:T(8,128)}, u32[]{:S(2)}) copy-start(s32[16,12]{1,0:T(8,128)} %param.16) | copy-start | bytes 2308
  67.7 33.2 %all-to-all-start.1 = ((s32[32,1,128]{2,1,0:T(1,128)}), s32[32,1,128]{2,1,0:T(1,128)S(1)}, u32[]{:S(2)}, u32[]{:S(2)}) async-start(s32[32,1,128]{2,1,0:T(1,128)} %reshape.253), calls=%async_computation.1 | async-start | bytes 32768 | tf_op jit(solution)/shard_map/all_to_all | solution.py:83
  78.1 7.4 %copy-start.5 = (bf16[2048,128]{1,0:T(8,128)(2,1)S(1)}, bf16[2048,128]{1,0:T(8,128)(2,1)}, u32[]{:S(2)}) copy-start(bf16[2048,128]{1,0:T(8,128)(2,1)} %get-tuple-element.13) | copy-start | bytes 1572868
  78.1 7.4 %copy-start.6 = (bf16[2048,128]{1,0:T(8,128)(2,1)S(1)}, bf16[2048,128]{1,0:T(8,128)(2,1)}, u32[]{:S(2)}) copy-start(bf16[2048,128]{1,0:T(8,128)(2,1)} %get-tuple-element.16) | copy-start | bytes 1572868
  84.7 0.8 copy-start.8
  101.0 6.8 %copy-start.9 = (bf16[256,172]{0,1:T(8,128)(2,1)S(1)}, bf16[256,172]{0,1:T(8,128)(2,1)}, u32[]{:S(2)}) copy-start(bf16[256,172]{0,1:T(8,128)(2,1)} %param.25) | copy-start | bytes 264196
  101.0 86.1 %all-to-all-start.2 = ((bf16[32,64,512]{2,1,0:T(8,128)(2,1)}), bf16[32,64,512]{2,1,0:T(8,128)(2,1)}, u32[]{:S(2)}, u32[]{:S(2)}) async-start(bf16[32,64,512]{2,1,0:T(8,128)(2,1)} %broadcast_select_fusion), calls=%async_computation.2 | async-start | bytes 4194304 | tf_op jit(solution)/shard_map/all_to_all | solution.py:82
  107.0 80.1 %all-gather.2.cloned.1.call-start = ((), (), s32[]{:S(2)}) async-start(), calls=%async_computation.6 | async-start | bytes 1310720 | tf_op jit(solution)/shard_map/all_gather | solution.py:87
  107.7 121.3 %reduce-scatter.8.cloned.1.call-start = ((), (), s32[]{:S(2)}) async-start(), calls=%async_computation.9 | async-start | bytes 901120 | tf_op jit(solution)/shard_map/reduce_scatter | solution.py:104
  191.3 3.9 %copy-start.4 = (f32[2048,1024]{1,0:T(8,128)}, f32[2048,1024]{1,0:T(8,128)S(1)}, u32[]{:S(2)}) copy-start(f32[2048,1024]{1,0:T(8,128)S(1)} %get-tuple-element.20) | copy-start | bytes 25165828
  191.3 1.3 copy-start.7
  192.6 1.6 copy-start.12
  192.6 3.2 copy-start.17
  195.2 0.6 copy-start.13
  205.7 68.2 %reduce-scatter.4.cloned.1.call-start = ((), (), s32[]{:S(2)}) async-start(), calls=%async_computation.7 | async-start | bytes 2621440 | tf_op jit(solution)/shard_map/reduce_scatter | solution.py:103
  217.1 56.8 %copy-start.14 = (f32[2048]{0:T(1024)S(1)}, f32[2048]{0:T(1024)}, u32[]{:S(2)}) copy-start(f32[2048]{0:T(1024)} %copy-done.13) | copy-start | bytes 24580
  217.1 56.8 %copy-start.15 = (f32[2048]{0:T(1024)S(1)}, f32[2048]{0:T(1024)}, u32[]{:S(2)}) copy-start(f32[2048]{0:T(1024)} %get-tuple-element.8) | copy-start | bytes 24580
  217.1 56.9 %copy-start.11 = (f32[1,32,64]{2,0,1:T(1,128)S(1)}, f32[1,32,64]{2,0,1:T(1,128)}, u32[]{:S(2)}) copy-start(f32[1,32,64]{2,0,1:T(1,128)} %get-tuple-element.18) | copy-start | bytes 24580
  217.1 57.1 %copy-start.19 = (f32[32]{0:T(128)S(1)}, f32[32]{0:T(128)}, u32[]{:S(2)}) copy-start(f32[32]{0:T(128)} %get-tuple-element.10) | copy-start | bytes 388
  217.1 112.0 %all-reduce.2.cloned.1.call-start = ((), (), s32[]{:S(2)}) async-start(), calls=%async_computation.10 | async-start | bytes 360448 | tf_op jit(solution)/shard_map/psum | solution.py:107
  229.0 137.9 %reduce-scatter.6.cloned.1.call-start = ((), (), s32[]{:S(2)}) async-start(), calls=%async_computation.8 | async-start | bytes 589824 | tf_op jit(solution)/shard_map/reduce_scatter | solution.py:106
Sparse Core Ops, SparseCore 0:
  109.3 55.8 all-gather.1
  205.8 23.0 reduce-scatter.7
  231.3 42.5 reduce-scatter.3
  276.9 52.2 all-reduce.1
  332.6 34.2 reduce-scatter.5
where the time goes:
time: 376 us; the launch traced here: 375 us
  waiting for transfers between devices  150 us (40%)
  blocking collectives  73.9 us (20%)
  local copies, waits for them, and re-layouts  68.5 us (18%)
  matrix products  35.3 us (9%)
  starting transfers between devices  19.3 us (5%)
  between operations  14.8 us (4%)
  other arithmetic  13.5 us (4%)
    all_gather x1, blocking collectives, shards(): lax.all_gather(w_second, 'rep', axis=0, tiled=True)  73.9 us
    psum x1, waiting for transfers between devices, shards(): grad_two = lax.psum(grad_two_rep, 'dom')  54.4 us
    reduce_scatter x1, waiting for transfers between devices, shards(): lax.psum_scatter(grad_one_full, 'rep', scatter_dimension=1, tiled=True)  44.9 us
    reduce_scatter x1, waiting for transfers between devices, shards(): lax.psum_scatter(grad_one_rep, 'dom', scatter_dimension=0, tiled=True)  37.7 us
    dot_general x2, matrix products, contract_rows(): lax.dot_general(left, right, (((0,), (0,)), ((), ())), preferred_element_...  13.2 us
    reduce_scatter x1, waiting for transfers between devices, shards(): lax.psum_scatter(grad_two_full, 'rep', scatter_dimension=0, tiled=True)  11.8 us
    gather x1, local copies, waits for them, and re-layouts, shards(): order = jnp.take(train_ids[0], shuffle[0], axis=0)  11.8 us
    gather x1, local copies, waits for them, and re-layouts, shards(): own_labels = jnp.take(labels, order, axis=0)  11.8 us
  transfers between devices with their start and end apart: 8, of which 4 were waited for; matrix products, arithmetic and copies ran while one was open for 23% of the time, Pallas kernels for 0%

commit v1 on v0

v1 whole, which is shorter than its diff:
```python
import math

import jax
import jax.numpy as jnp
from jax import lax
from jax.experimental import pallas as pl
from jax.experimental.pallas import tpu as pltpu
from jax.sharding import PartitionSpec as P

BOTH = ("dom", "rep")


def tile_sum_kernel(cols, tiles, table, *rest):
    base, out = (rest[0], rest[1]) if len(rest) == 2 else (None, rest[0])
    step = pl.program_id(0)
    block, depth = tiles.shape[0], tiles.shape[1]
    size = tiles.shape[2]
    for i in range(block):
        left = jnp.concatenate([tiles[i, k] for k in range(depth)], axis=1)
        right = jnp.concatenate(
            [table[cols[(step * block + i) * depth + k]] for k in range(depth)], axis=0
        )
        total = jnp.dot(left, right, preferred_element_type=jnp.float32)
        if base is not None:
            total = total + base[pl.ds(i * size, size), :]
        out[pl.ds(i * size, size), :] = total.astype(out.dtype)


def tile_sum(tiles, cols, table, base, dtype):
    count, depth, size, _ = tiles.shape
    width = table.shape[-1]
    block = math.gcd(count, max(1, 48 // depth))
    specs = [
        pl.BlockSpec((block, depth, size, size), lambda s, c: (s, 0, 0, 0)),
        pl.BlockSpec(table.shape, lambda s, c: (0, 0, 0)),
    ]
    operands = [tiles, table]
    if base is not None:
        specs.append(pl.BlockSpec((block * size, width), lambda s, c: (s, 0)))
        operands.append(base)
    return pl.pallas_call(
        tile_sum_kernel,
        grid_spec=pltpu.PrefetchScalarGridSpec(
            num_scalar_prefetch=1,
            grid=(count // block,),
            in_specs=specs,
            out_specs=pl.BlockSpec((block * size, width), lambda s, c: (s, 0)),
        ),
        out_shape=jax.ShapeDtypeStruct((count * size, width), dtype),
        name="tile_sum",
    )(cols.reshape(-1), *operands)


def pick_rows_kernel(order, hops, last, out):
    rows = hops.shape[1]
    ids = order[...]
    nodes = lax.broadcasted_iota(jnp.int32, (ids.shape[0], rows), 1)
    picks = jnp.where(ids == nodes, 1.0, 0.0).astype(jnp.bfloat16)
    table = jnp.concatenate([hops[0], hops[1], hops[2], last[...]], axis=1)
    out[...] = jnp.dot(picks, table, preferred_element_type=jnp.float32).astype(out.dtype)


def pick_rows(order, hops, last):
    slots = order.shape[0]
    width = hops.shape[2]
    block = 256
    return pl.pallas_call(
        pick_rows_kernel,
        grid=(slots // block,),
        in_specs=[
            pl.BlockSpec((block, 1), lambda s: (s, 0)),
            pl.BlockSpec(hops.shape, lambda s: (0, 0, 0)),
            pl.BlockSpec(last.shape, lambda s: (0, 0)),
        ],
        out_specs=pl.BlockSpec((block, 4 * width), lambda s: (s, 0)),
        out_shape=jax.ShapeDtypeStruct((slots, 4 * width), hops.dtype),
        name="pick_rows",
    )(order[:, None], hops, last)


def take_ints(tables, index, lanes):
    groups = tables[0].shape[0] // lanes
    parts = []
    for table in tables:
        grid = table.reshape(groups, lanes)
        parts += [grid // 128, grid % 128]
    stacked = jnp.concatenate(parts, axis=0).astype(jnp.bfloat16)
    low, high = index % lanes, index // lanes
    onehot = (lax.broadcasted_iota(jnp.int32, (lanes, index.shape[0]), 0) == low[None, :]).astype(jnp.bfloat16)
    found = jnp.dot(stacked, onehot, preferred_element_type=jnp.float32)
    found = found.reshape(len(tables), 2, groups, index.shape[0])
    mask = lax.broadcasted_iota(jnp.int32, (groups, index.shape[0]), 0) == high[None, :]
    sums = jnp.sum(jnp.where(mask[None, None], found, 0.0), axis=2).astype(jnp.int32)
    return [sums[t, 0] * 128 + sums[t, 1] for t in range(len(tables))]


def gather_by_exchange(value, axes, count):
    copies = jnp.broadcast_to(value, (count,) + value.shape[1:])
    return lax.all_to_all(copies, axes, split_axis=0, concat_axis=0, tiled=True)


def contract_rows(left, right):
    return lax.dot_general(
        left, right, (((0,), (0,)), ((), ())), preferred_element_type=jnp.float32
    )


def shards(
    hop_feats,
    adj_local,
    local_cols,
    adj_halo,
    halo_cols,
    boundary_rows,
    train_ids,
    shuffle,
    labels,
    labelled,
    w_first,
    w_second,
):
    num_dom = lax.axis_size("dom")
    num_rep = lax.axis_size("rep")
    devices = num_dom * num_rep
    tile = adj_local.shape[-1]
    row_tiles = adj_local.shape[0]
    width = hop_feats.shape[2]
    slots = shuffle.shape[1]
    share = slots // devices
    inner = w_first.shape[0]
    hop_two = hop_feats[2]
    sent = hop_two.at[boundary_rows[0]].get(mode="promise_in_bounds")
    own = jnp.concatenate([w_first, w_second.T], axis=0)
    halo = lax.all_to_all(sent, BOTH, split_axis=0, concat_axis=0, tiled=True)
    rep_at = lax.axis_index("rep")
    pieces = jnp.stack(
        [own]
        + [
            lax.ppermute(own, "rep", [(i, (i + s) % num_rep) for i in range(num_rep)])
            for s in range(1, num_rep)
        ]
    )
    packed = jnp.concatenate(
        [
            lax.dynamic_index_in_dim(pieces, (rep_at - i + num_rep) % num_rep, 0, keepdims=False)
            for i in range(num_rep)
        ],
        axis=1,
    )
    near_sum = tile_sum(
        adj_local, local_cols, hop_two.reshape(row_tiles, tile, width), None, jnp.float32
    )
    (order,) = take_ints([train_ids[0]], shuffle[0], tile)
    targets, marks = take_ints([labels, labelled], order, tile)
    marks = marks.astype(jnp.float32)
    next_hop = tile_sum(adj_halo, halo_cols, halo.reshape(-1, tile, width), near_sum, jnp.bfloat16)
    batch = pick_rows(order, hop_feats, next_hop)
    first_whole, second_t = packed[:inner], packed[inner:]
    hidden_units = first_whole.shape[1]
    classes = second_t.shape[0]

    pre = jnp.dot(batch, first_whole, preferred_element_type=jnp.float32)
    pre3 = pre.reshape(devices, share, hidden_units)
    part_mean = jnp.mean(pre3, axis=1)
    part_dev = pre3 - part_mean[:, None, :]
    part_m2 = jnp.mean(part_dev * part_dev, axis=1)
    part_count = jnp.sum(marks.reshape(devices, share), axis=1)
    lane = 128
    count_cols = jnp.broadcast_to(part_count[:, None], (devices, lane))
    stats = jnp.concatenate([part_mean, part_m2, count_cols], axis=1)
    got = lax.all_to_all(stats, BOTH, split_axis=0, concat_axis=0, tiled=True)
    means = got[:, :hidden_units]
    mean = jnp.mean(means, axis=0, keepdims=True)
    off = means - mean
    var = jnp.mean(got[:, hidden_units : 2 * hidden_units] + off * off, axis=0, keepdims=True)
    total = jnp.maximum(jnp.sum(got[:, 2 * hidden_units :], axis=0, keepdims=True), 1.0)
    mine = jnp.concatenate([mean, lax.rsqrt(var + 1e-05), 1.0 / total], axis=1)
    every = gather_by_exchange(mine, BOTH, devices)
    mu = every[:, None, :hidden_units]
    rstd = every[:, None, hidden_units : 2 * hidden_units]
    inv_count = every[:, 2 * hidden_units]

    normed3 = (pre3 - mu) * rstd
    normed = normed3.reshape(slots, hidden_units)
    hidden = jnp.maximum(normed, 0.0).astype(jnp.bfloat16)
    logits = lax.dot_general(
        second_t, hidden, (((1,), (1,)), ((), ())), preferred_element_type=jnp.float32
    )
    row_max = jnp.max(logits, axis=0, keepdims=True)
    expos = jnp.exp(logits - row_max)
    totals = jnp.sum(expos, axis=0, keepdims=True)
    onehot = (lax.broadcasted_iota(jnp.int32, logits.shape, 0) == targets[None, :]).astype(jnp.float32)
    cross = jnp.log(totals[0]) + row_max[0] - jnp.sum(onehot * logits, axis=0)
    scale = marks * jnp.broadcast_to(inv_count[:, None], (devices, share)).reshape(slots)
    dlogits = ((expos / totals - onehot) * scale[None, :]).astype(jnp.bfloat16)
    dlogits = lax.optimization_barrier(dlogits)
    grad_two_full = lax.dot_general(
        hidden, dlogits, (((0,), (1,)), ((), ())), preferred_element_type=jnp.float32
    )
    g_two = grad_two_full.astype(jnp.bfloat16).reshape(num_rep, -1, classes)

    dhidden = contract_rows(dlogits, second_t)
    masked3 = jnp.where(normed > 0, dhidden, 0.0).reshape(devices, share, hidden_units)
    part_grad = jnp.mean(masked3, axis=1)
    part_proj = jnp.mean(masked3 * normed3, axis=1)
    losses = jnp.sum((marks * cross).reshape(devices, share), axis=1) / jnp.maximum(part_count, 1.0)
    loss_cols = jnp.broadcast_to(losses[:, None], (devices, lane))
    sums = lax.all_to_all(
        jnp.concatenate([part_grad, part_proj, loss_cols], axis=1),
        BOTH, split_axis=0, concat_axis=0, tiled=True,
    )
    loss = sums[:, 2 * hidden_units].reshape(1, devices)
    back = gather_by_exchange(
        jnp.mean(sums[:, : 2 * hidden_units], axis=0, keepdims=True), BOTH, devices
    )
    back, g_two = lax.optimization_barrier((back, g_two))
    g_two = lax.all_to_all(g_two, "rep", split_axis=0, concat_axis=0, tiled=True)
    mean_grad = back[:, None, :hidden_units]
    mean_proj = back[:, None, hidden_units:]
    dpre = ((masked3 - mean_grad - normed3 * mean_proj) * rstd).astype(jnp.bfloat16)
    grad_one_full = contract_rows(batch, dpre.reshape(slots, hidden_units))
    g_one = grad_one_full.astype(jnp.bfloat16).reshape(num_dom, -1, hidden_units)
    g_two = jnp.sum(g_two.astype(jnp.float32), axis=0).astype(jnp.bfloat16)
    span = hidden_units // num_rep
    g_two = jnp.pad(g_two, ((0, 0), (0, span - classes)))
    g_two = g_two.reshape(num_dom, num_rep, -1, span)
    short = g_two.shape[2]
    g_two = jnp.concatenate([g_two[:, i] for i in range(num_rep)], axis=2)
    long = g_one.shape[1]
    both = lax.all_to_all(
        jnp.concatenate([g_one, g_two], axis=1), "dom", split_axis=0, concat_axis=0, tiled=True
    )
    both = jnp.sum(both.astype(jnp.float32), axis=0)
    blocks = jnp.stack([both[:long, i * span : (i + 1) * span] for i in range(num_rep)])
    grad_one = lax.dynamic_index_in_dim(blocks, rep_at, 0, keepdims=False)
    for s in range(1, num_rep):
        block = lax.dynamic_index_in_dim(blocks, (rep_at + s) % num_rep, 0, keepdims=False)
        grad_one = grad_one + lax.ppermute(
            block, "rep", [(i, (i + s) % num_rep) for i in range(num_rep)]
        )
    g_two = jnp.concatenate(
        [both[long:, i * span : i * span + classes] for i in range(num_rep)], axis=0
    )
    grad_two = gather_by_exchange(g_two[None], "dom", num_dom).reshape(-1, classes)
    return (next_hop, loss, grad_one, grad_two)


def solution(mesh):
    placed = (
        P(None, BOTH, None),
        P(BOTH, None, None, None),
        P(BOTH, None),
        P(BOTH, None, None, None),
        P(BOTH, None),
        P(BOTH, None),
        P(BOTH, None),
        P(BOTH, None),
        P(BOTH),
        P(BOTH),
        P(None, "rep"),
        P("rep", None),
    )
    return jax.shard_map(
        shards,
        mesh=mesh,
        in_specs=placed,
        out_specs=(P(BOTH, None), P(BOTH, None), P("dom", "rep"), P("rep", None)),
        check_vma=False,
    )
```

time: 376 us -> 189 us (0.50)
  waiting for transfers between devices: 150 us -> 53.6 us
  local copies, waits for them, and re-layouts: 68.5 us -> 17.3 us
  blocking collectives: 73.9 us -> 27.7 us
  Pallas kernels: 0 us -> 20.5 us
  matrix products: 35.3 us -> 17 us
  between operations: 14.8 us -> 1.32 us
  starting transfers between devices: 19.3 us -> 30.8 us
  other arithmetic: 13.5 us -> 20.2 us
    reduce_scatter x3 -> x0, waiting for transfers between devices: 94.4 us -> none  [the longest x1 44.9 us: shards(): lax.psum_scatter(grad_one_full, 'rep', scatter_dimension=1, tiled=True)]
    all_gather x1 -> x0, blocking collectives: 73.9 us -> none  [shards(): lax.all_gather(w_second, 'rep', axis=0, tiled=True)]
    gather x7 -> x1, local copies, waits for them, and re-layouts: 57.9 us -> 1.91 us  [shards(): sent = hop_two.at[boundary_rows[0]].get(mode='promise_in_bounds')]
    psum x1 -> x0, waiting for transfers between devices: 54.4 us -> none  [shards(): grad_two = lax.psum(grad_two_rep, 'dom')]
    all_to_all x3 -> x6, waiting for transfers between devices: 0.01 us -> 52.6 us  [the longest x3 22.3 us: gather_by_exchange(): return lax.all_to_all(copies, axes, split_axis=0, concat_axis=0, tiled=True)]
    all_to_all x0 -> x2, blocking collectives: none -> 27.7 us  [the longest x1 14.7 us: shards(): got = lax.all_to_all(stats, BOTH, split_axis=0, concat_axis=0, tiled=True)]
    pallas_call x0 -> x3, Pallas kernels: none -> 20.5 us  [the longest x2 11.3 us: tile_sum(): pl.pallas_call(tile_sum_kernel, grid_spec=pltpu.PrefetchScalarGridSpec(nu...]
    dot_general x5, matrix products: 22.2 us -> 7.67 us  [the longest x1 3.1 us: shards(): lax.dot_general(hidden, dlogits, (((0,), (1,)), ((), ())), preferred_elem...]
  transfers between devices with their start and end apart: 8 -> 12, of which waited for: 4 -> 7; matrix products, arithmetic and copies ran while one was open for 23% -> 13% of each run, Pallas kernels for 0% -> 11%
where the time goes in v1:
time: 189 us; the launch traced here: 188 us
  waiting for transfers between devices  53.6 us (28%)
  starting transfers between devices  30.8 us (16%)
  blocking collectives  27.7 us (15%)
  Pallas kernels  20.5 us (11%)
  other arithmetic  20.2 us (11%)
  local copies, waits for them, and re-layouts  17.3 us (9%)
  matrix products  17 us (9%)
    all_to_all x3, waiting for transfers between devices, gather_by_exchange(): return lax.all_to_all(copies, axes, split_axis=0, concat_axis=0, tiled=True)  22.3 us
    all_to_all x1, waiting for transfers between devices, shards(): lax.all_to_all(jnp.concatenate([g_one, g_two], axis=1), 'dom', split_axis...  16.1 us
    all_to_all x1, blocking collectives, shards(): got = lax.all_to_all(stats, BOTH, split_axis=0, concat_axis=0, tiled=True)  14.7 us
    all_to_all x1, blocking collectives, shards(): lax.all_to_all(jnp.concatenate([part_grad, part_proj, loss_cols], axis=1)...  13 us
    all_to_all x1, waiting for transfers between devices, shards(): halo = lax.all_to_all(sent, BOTH, split_axis=0, concat_axis=0, tiled=True)  12.2 us
    pallas_call x2, Pallas kernels, tile_sum(): pl.pallas_call(tile_sum_kernel, grid_spec=pltpu.PrefetchScalarGridSpec(nu...  11.3 us
    dot_general x2, matrix products, contract_rows(): lax.dot_general(left, right, (((0,), (0,)), ((), ())), preferred_element_...  9.31 us
    all_to_all x3, starting transfers between devices, gather_by_exchange(): return lax.all_to_all(copies, axes, split_axis=0, concat_axis=0, tiled=True)  9.14 us
  transfers between devices with their start and end apart: 12, of which 7 were waited for; matrix products, arithmetic and copies ran while one was open for 13% of the time, Pallas kernels for 11%

profile of v1, /device:TPU:0, one launch (start us, length us, event | category | flops | bytes accessed | tf_op | source)
XLA Modules:
  0.0 188.4 jit_solution(2277560799935704261)
XLA Ops:
  0.7 1.1 fusion.45
  1.8 4.1 %collective-permute-start.1 = (bf16[684,256]{1,0:T(8,128)(2,1)S(1)}, bf16[684,256]{1,0:T(8,128)(2,1)S(1)}, u32[]{:S(2)}, u32[]{:S(2)}) collective-permute-start(bf16[684,256]{1,0:T(8,128)(2,1)S(1)} %get-tuple-element.35), channel_id=1, source_target_pairs={{0,2},{1,3},{2,0},{3,1},{4,6},{5,7},{6,4},{7,5},{8,10},{9,11},{10,... | collective-permute-start | bytes 1050632 | tf_op jit(solution)/shard_map/ppermute | solution.py:139
  5.9 1.6 collective-permute-start
  7.5 2.2 %collective-permute-start.2 = (bf16[684,256]{1,0:T(8,128)(2,1)S(1)}, bf16[684,256]{1,0:T(8,128)(2,1)S(1)}, u32[]{:S(2)}, u32[]{:S(2)}) collective-permute-start(bf16[684,256]{1,0:T(8,128)(2,1)S(1)} %get-tuple-element.35), channel_id=1, source_target_pairs={{0,3},{1,0},{2,1},{3,2},{4,7},{5,4},{6,5},{7,6},{8,11},{9,8},{10,9... | collective-permute-start | bytes 1050632 | tf_op jit(solution)/shard_map/ppermute | solution.py:139
  9.7 0.7 compare_select_fusion.4
  10.4 2.0 %fusion.48 = (bf16[1,2048,128]{2,1,0:T(8,128)(2,1)}, bf16[2048,128]{1,0:T(8,128)(2,1)S(1)}) fusion(bf16[3,2048,128]{2,1,0:T(8,128)(2,1)} %hops.1), kind=kLoop, calls=%fused_computation.161 | loop fusion | bytes 1572864 | tf_op jit(solution)/shard_map/slice | solution.py:131
  12.4 1.9 %gather_fusion = bf16[512,128]{1,0:T(8,128)(2,1)} fusion(bf16[2048,128]{1,0:T(8,128)(2,1)S(1)} %get-tuple-element.29, s32[1024]{0:T(1024)S(1)} %pad_clamp_fusion), kind=kCustom, calls=%fused_computation | custom fusion | bytes 264192 | tf_op jit(solution)/shard_map/gather | solution.py:132
  14.3 2.8 %all-to-all-start = ((bf16[32,16,128]{2,1,0:T(8,128)(2,1)}), bf16[32,16,128]{2,1,0:T(8,128)(2,1)S(1)}, u32[]{:S(2)}, u32[]{:S(2)}) async-start(bf16[32,16,128]{2,1,0:T(8,128)(2,1)} %bitcast.3), calls=%async_computation | async-start | bytes 262144 | tf_op jit(solution)/shard_map/all_to_all | solution.py:134
  17.2 0.7 reshape.367.cols
  20.1 0.7 fusion.46
  21.0 1.4 copy.40.order
  22.4 6.3 %tile_sum.2.rest_0_ = f32[2048,128]{1,0:T(8,128)} custom-call(s32[192]{0:T(256)} %reshape.367.cols, bf16[16,12,128,128]{3,2,1,0:T(8,128)(2,1)} %tiles.2, bf16[16,128,128]{2,1,0:T(8,128)(2,1)} %bitcast.212), custom_call_target="tpu_custom_call" | custom-call | tf_op jit(solution)/shard_map/tile_sum/pallas_call | solution.py:41
  28.7 12.2 %all-to-all-done = bf16[32,16,128]{2,1,0:T(8,128)(2,1)S(1)} async-done(((bf16[32,16,128]{2,1,0:T(8,128)(2,1)}), bf16[32,16,128]{2,1,0:T(8,128)(2,1)S(1)}, u32[]{:S(2)}, u32[]{:S(2)}) %all-to-all-start) | async-done | bytes 131104 | tf_op jit(solution)/shard_map/all_to_all | solution.py:134
  41.0 0.7 copy-done.4
  41.6 5.0 %tile_sum.3.last = bf16[2048,128]{1,0:T(8,128)(2,1)} custom-call(s32[64]{0:T(128)} %reshape.365.cols, bf16[16,4,128,128]{3,2,1,0:T(8,128)(2,1)} %tiles.3, bf16[4,128,128]{2,1,0:T(8,128)(2,1)} %bitcast.224, f32[2048,128]{1,0:T(8,128)} %tile_sum.2.rest_0_), custom_call_target="tpu_custom_call" | custom-call | tf_op jit(solution)/shard_map/tile_sum/pallas_call | solution.py:41
  46.6 9.1 %pick_rows.1 = bf16[2048,512]{1,0:T(8,128)(2,1)} custom-call(s32[2048,1]{1,0:T(8,128)} %copy.40.order, bf16[3,2048,128]{2,1,0:T(8,128)(2,1)} %hops.1, bf16[2048,128]{1,0:T(8,128)(2,1)} %tile_sum.3.last), custom_call_target="tpu_custom_call" | custom-call | tf_op jit(solution)/shard_map/pick_rows/pallas_call | solution.py:67
  56.3 1.3 copy-done.2
  57.6 2.4 %bitcast_reduce_fusion.1 = (f32[32,1024]{1,0:T(8,128)S(1)}, f32[2048,1024]{1,0:T(8,128)S(1)}) fusion(bf16[2048,512]{1,0:T(8,128)(2,1)S(1)} %copy-done.2, bf16[684,1024]{1,0:T(8,128)(2,1)S(1)} %pad_maximum_fusion.1), kind=kOutput, calls=%fused_computation.13 | convolution fusion | flops 2149548032 | bytes 11665408 | tf_op jit(solution)/shard_map/dot_general | solution.py:162
  60.0 1.5 fusion.4
  61.5 1.7 copy-done
  63.5 14.7 %all_to_all.66 = f32[32,1,2176]{2,1,0:T(1,128)S(1)} all-to-all(f32[32,1,2176]{2,1,0:T(1,128)S(1)} %all_to_all.45), channel_id=1, replica_groups=mesh['dom'=8,'rep'=4] {'dom','rep'}, dimensions={0} | all-to-all | bytes 557056 | tf_op jit(solution)/shard_map/all_to_all | solution.py:171
  78.4 0.9 broadcast_in_dim.44
  79.2 3.0 %all-to-all-start.2 = ((f32[32,1,2176]{2,1,0:T(1,128)}), f32[32,1,2176]{2,1,0:T(1,128)S(1)}, u32[]{:S(2)}, u32[]{:S(2)}) async-start(f32[32,1,2176]{2,1,0:T(1,128)} %broadcast_in_dim.44), calls=%async_computation.2 | async-start | bytes 557056 | tf_op jit(solution)/shard_map/all_to_all | solution.py:99
  82.3 10.2 %all-to-all-done.2 = f32[32,1,2176]{2,1,0:T(1,128)S(1)} async-done(((f32[32,1,2176]{2,1,0:T(1,128)}), f32[32,1,2176]{2,1,0:T(1,128)S(1)}, u32[]{:S(2)}, u32[]{:S(2)}) %all-to-all-start.2) | async-done | bytes 278560 | tf_op jit(solution)/shard_map/all_to_all | solution.py:99
  92.8 4.8 %maximum_convert_fusion = bf16[2048,1024]{1,0:T(8,128)(2,1)S(1)} fusion(f32[2048,1024]{1,0:T(8,128)} %copy-done, f32[32,1024]{1,0:T(8,128)S(1)} %get-tuple-element.45, f32[32,1024]{1,0:T(8,128)S(1)} %get-tuple-element.44), kind=kLoop, calls=%fused_computation.17 | loop fusion | flops 8388608 | bytes 12845056 | tf_op jit(solution)/shard_map/convert_element_type | solution.py:185
  97.6 1.6 fusion.52
  100.5 7.0 %bitcast_reduce_fusion = (f32[32,1024]{1,0:T(8,128)S(1)}, f32[32,1024]{1,0:T(8,128)S(1)}, f32[2048,1024]{1,0:T(8,128)}) fusion(f32[2048,1024]{1,0:T(8,128)} %copy-done, f32[32,1024]{1,0:T(8,128)S(1)} %get-tuple-element.45, f32[32,1024]{1,0:T(8,128)S(1)} %get-tuple-element.44, bf16[172,2048]{1,0:T(8,128)(2,1)S(1)} %multiply_convert_fusion, ...), kind=kOutput, calls=%fused_computation.8 | convolution fusion | flops 740229120 | bytes 18358272 | tf_op jit(solution)/shard_map/dot_general | solution.py:103
  107.8 13.0 %all_to_all.67 = f32[32,1,2176]{2,1,0:T(1,128)S(1)} all-to-all(f32[32,1,2176]{2,1,0:T(1,128)S(1)} %all_to_all.50), channel_id=1, replica_groups=mesh['dom'=8,'rep'=4] {'dom','rep'}, dimensions={0} | all-to-all | bytes 557056 | tf_op jit(solution)/shard_map/all_to_all | solution.py:208
  120.9 0.8 broadcast_in_dim.49
  121.7 2.8 %all-to-all-start.4 = ((f32[32,1,2048]{2,1,0:T(1,128)}), f32[32,1,2048]{2,1,0:T(1,128)S(1)}, u32[]{:S(2)}, u32[]{:S(2)}) async-start(f32[32,1,2048]{2,1,0:T(1,128)} %broadcast_in_dim.49), calls=%async_computation.4 | async-start | bytes 524288 | tf_op jit(solution)/shard_map/all_to_all | solution.py:99
  124.5 3.1 %convolution_convert_fusion.1 = bf16[1024,172]{0,1:T(8,128)(2,1)S(1)} fusion(bf16[2048,1024]{1,0:T(8,128)(2,1)} %copy-done.1, bf16[172,2048]{1,0:T(8,128)(2,1)S(1)} %multiply_convert_fusion), kind=kOutput, calls=%fused_computation.28 | convolution fusion | flops 721596416 | bytes 5251072 | tf_op jit(solution)/shard_map/dot_general | solution.py:197
  127.8 6.9 %all-to-all-done.4 = f32[32,1,2048]{2,1,0:T(1,128)S(1)} async-done(((f32[32,1,2048]{2,1,0:T(1,128)}), f32[32,1,2048]{2,1,0:T(1,128)S(1)}, u32[]{:S(2)}, u32[]{:S(2)}) %all-to-all-start.4) | async-done | bytes 262176 | tf_op jit(solution)/shard_map/all_to_all | solution.py:99
  134.9 0.8 copy.41
  135.6 3.5 %all-to-all-start.5 = ((bf16[4,256,172]{1,2,0:T(8,128)(2,1)}), bf16[4,256,172]{1,2,0:T(8,128)(2,1)S(1)}, u32[]{:S(2)}, u32[]{:S(2)}) async-start(bf16[4,256,172]{1,2,0:T(8,128)(2,1)} %copy.41), calls=%async_computation.5 | async-start | bytes 720896 | tf_op jit(solution)/shard_map/all_to_all | solution.py:217
  139.1 7.4 %fusion = bf16[2048,1024]{1,0:T(8,128)(2,1)S(1)} fusion(f32[2048,1024]{1,0:T(8,128)} %copy-done, f32[2048,1024]{1,0:T(8,128)} %get-tuple-element.67, f32[32,1024]{1,0:T(8,128)S(1)} %get-tuple-element.50, f32[32,1024]{1,0:T(8,128)S(1)} %get-tuple-element.49, f32[32,1024]{1,0:T(8,128)S(1)} %get-tuple-element.45, f32[32,1024]{1,0:T(8,128)S(1)} %get-tuple-element.44), kind=kLoop, calls=%fused_computation.3 | loop fusion | flops 18874368 | bytes 21495808 | tf_op jit(solution)/shard_map/convert_element_type | solution.py:220
  146.5 2.3 %convolution_convert_fusion = bf16[512,1024]{1,0:T(8,128)(2,1)S(1)} fusion(bf16[2048,512]{1,0:T(8,128)(2,1)S(1)} %copy-done.3, bf16[2048,1024]{1,0:T(8,128)(2,1)S(1)} %fusion), kind=kOutput, calls=%fused_computation.20 | convolution fusion | flops 2148007936 | bytes 7340032 | tf_op jit(solution)/shard_map/dot_general | solution.py:103
  148.9 2.0 %all-to-all-done.5 = bf16[4,256,172]{1,2,0:T(8,128)(2,1)S(1)} async-done(((bf16[4,256,172]{1,2,0:T(8,128)(2,1)}), bf16[4,256,172]{1,2,0:T(8,128)(2,1)S(1)}, u32[]{:S(2)}, u32[]{:S(2)}) %all-to-all-start.5) | async-done | bytes 352288 | tf_op jit(solution)/shard_map/all_to_all | solution.py:217
  151.0 1.1 maximum_maximum_fusion
  152.2 3.6 %all-to-all-start.6 = ((bf16[8,72,1024]{2,1,0:T(8,128)(2,1)}), bf16[8,72,1024]{2,1,0:T(8,128)(2,1)S(1)}, u32[]{:S(2)}, u32[]{:S(2)}) async-start(bf16[8,72,1024]{2,1,0:T(8,128)(2,1)} %maximum_maximum_fusion), calls=%async_computation.6 | async-start | bytes 2359296 | tf_op jit(solution)/shard_map/all_to_all | solution.py:230
  155.7 0.6 slice_reduce_fusion.2
  156.4 16.1 %all-to-all-done.6 = bf16[8,72,1024]{2,1,0:T(8,128)(2,1)S(1)} async-done(((bf16[8,72,1024]{2,1,0:T(8,128)(2,1)}), bf16[8,72,1024]{2,1,0:T(8,128)(2,1)S(1)}, u32[]{:S(2)}, u32[]{:S(2)}) %all-to-all-start.6) | async-done | bytes 1179680 | tf_op jit(solution)/shard_map/all_to_all | solution.py:230
  172.8 3.8 %collective-permute-start.5 = (f32[64,256]{1,0:T(8,128)S(1)}, f32[64,256]{1,0:T(8,128)S(1)}, u32[]{:S(2)}, u32[]{:S(2)}) collective-permute-start(f32[64,256]{1,0:T(8,128)S(1)} %get-tuple-element.47), channel_id=1, source_target_pairs={{0,3},{1,0},{2,1},{3,2},{4,7},{5,4},{6,5},{7,6},{8,11},{9,8},{10,9... | collective-permute-start | bytes 196616 | tf_op jit(solution)/shard_map/ppermute | solution.py:238
  176.6 0.7 broadcast_in_dim.50
  177.4 3.4 %all-to-all-start.7 = ((f32[8,32,172]{2,1,0:T(8,128)}), f32[8,32,172]{2,1,0:T(8,128)S(1)}, u32[]{:S(2)}, u32[]{:S(2)}) async-start(f32[8,32,172]{2,1,0:T(8,128)} %broadcast_in_dim.50), calls=%async_computation.7 | async-start | bytes 524288 | tf_op jit(solution)/shard_map/all_to_all | solution.py:99
  180.8 1.0 collective-permute-done.4
  181.8 0.6 fusion.15
  182.4 5.2 %all-to-all-done.7 = f32[8,32,172]{2,1,0:T(8,128)S(1)} async-done(((f32[8,32,172]{2,1,0:T(8,128)}), f32[8,32,172]{2,1,0:T(8,128)S(1)}, u32[]{:S(2)}, u32[]{:S(2)}) %all-to-all-start.7) | async-done | bytes 176160 | tf_op jit(solution)/shard_map/all_to_all | solution.py:99
  187.6 0.8 copy.47
  (97 shorter events, 6.2 us)
Async XLA Ops:
  0.6 16.5 %copy-start.6 = (s32[16,12]{1,0:T(8,128)S(1)}, s32[16,12]{1,0:T(8,128)}, u32[]{:S(2)}) copy-start(s32[16,12]{1,0:T(8,128)} %param.14) | copy-start | bytes 2308
  0.6 17.2 %copy-start.10 = (s32[16,4]{0,1:T(4,128)S(1)}, s32[16,4]{0,1:T(4,128)}, u32[]{:S(2)}) copy-start(s32[16,4]{0,1:T(4,128)} %param.16) | copy-start | bytes 772
  0.7 17.9 %copy-start.7 = (s32[1,2048]{1,0:T(1,128)S(1)}, s32[1,2048]{1,0:T(1,128)}, u32[]{:S(2)}) copy-start(s32[1,2048]{1,0:T(1,128)} %param.18) | copy-start | bytes 24580
  0.7 17.9 %copy-start.5 = (s32[1,2048]{1,0:T(1,128)S(1)}, s32[1,2048]{1,0:T(1,128)}, u32[]{:S(2)}) copy-start(s32[1,2048]{1,0:T(1,128)} %param.19) | copy-start | bytes 24580
  0.7 18.5 %copy-start.8 = (s32[2048]{0:T(1024)S(1)}, s32[2048]{0:T(1024)}, u32[]{:S(2)}) copy-start(s32[2048]{0:T(1024)} %param.20) | copy-start | bytes 24580
  0.7 18.5 %copy-start.9 = (s32[2048]{0:T(1024)S(1)}, s32[2048]{0:T(1024)}, u32[]{:S(2)}) copy-start(s32[2048]{0:T(1024)} %param.21) | copy-start | bytes 24580
  1.8 54.0 %collective-permute-start.1 = (bf16[684,256]{1,0:T(8,128)(2,1)S(1)}, bf16[684,256]{1,0:T(8,128)(2,1)S(1)}, u32[]{:S(2)}, u32[]{:S(2)}) collective-permute-start(bf16[684,256]{1,0:T(8,128)(2,1)S(1)} %get-tuple-element.35), channel_id=1, source_target_pairs={{0,2},{1,3},{2,0},{3,1},{4,6},{5,7},{6,4},{7,5},{8,10},{9,11},{10,... | collective-permute-start | bytes 1050632 | tf_op jit(solution)/shard_map/ppermute | solution.py:139
  5.9 49.9 %collective-permute-start = (bf16[684,256]{1,0:T(8,128)(2,1)S(1)}, bf16[684,256]{1,0:T(8,128)(2,1)S(1)}, u32[]{:S(2)}, u32[]{:S(2)}) collective-permute-start(bf16[684,256]{1,0:T(8,128)(2,1)S(1)} %get-tuple-element.35), channel_id=1, source_target_pairs={{0,1},{1,2},{2,3},{3,0},{4,5},{5,6},{6,7},{7,4},{8,9},{9,10},{10,1... | collective-permute-start | bytes 1050632 | tf_op jit(solution)/shard_map/ppermute | solution.py:139
  7.5 48.3 %collective-permute-start.2 = (bf16[684,256]{1,0:T(8,128)(2,1)S(1)}, bf16[684,256]{1,0:T(8,128)(2,1)S(1)}, u32[]{:S(2)}, u32[]{:S(2)}) collective-permute-start(bf16[684,256]{1,0:T(8,128)(2,1)S(1)} %get-tuple-element.35), channel_id=1, source_target_pairs={{0,3},{1,0},{2,1},{3,2},{4,7},{5,4},{6,5},{7,6},{8,11},{9,8},{10,9... | collective-permute-start | bytes 1050632 | tf_op jit(solution)/shard_map/ppermute | solution.py:139
  14.3 26.7 %all-to-all-start = ((bf16[32,16,128]{2,1,0:T(8,128)(2,1)}), bf16[32,16,128]{2,1,0:T(8,128)(2,1)S(1)}, u32[]{:S(2)}, u32[]{:S(2)}) async-start(bf16[32,16,128]{2,1,0:T(8,128)(2,1)} %bitcast.3), calls=%async_computation | async-start | bytes 262144 | tf_op jit(solution)/shard_map/all_to_all | solution.py:134
  41.0 0.7 copy-start.4
  56.0 1.6 copy-start.2
  60.0 3.2 %copy-start = (f32[2048,1024]{1,0:T(8,128)}, f32[2048,1024]{1,0:T(8,128)S(1)}, u32[]{:S(2)}) copy-start(f32[2048,1024]{1,0:T(8,128)S(1)} %get-tuple-element.64) | copy-start | bytes 25165828
  79.2 13.2 %all-to-all-start.2 = ((f32[32,1,2176]{2,1,0:T(1,128)}), f32[32,1,2176]{2,1,0:T(1,128)S(1)}, u32[]{:S(2)}, u32[]{:S(2)}) async-start(f32[32,1,2176]{2,1,0:T(1,128)} %broadcast_in_dim.44), calls=%async_computation.2 | async-start | bytes 557056 | tf_op jit(solution)/shard_map/all_to_all | solution.py:99
  97.6 1.9 %copy-start.1 = (bf16[2048,1024]{1,0:T(8,128)(2,1)}, bf16[2048,1024]{1,0:T(8,128)(2,1)S(1)}, u32[]{:S(2)}) copy-start(bf16[2048,1024]{1,0:T(8,128)(2,1)S(1)} %maximum_convert_fusion) | copy-start | bytes 12582916
  121.7 13.0 %all-to-all-start.4 = ((f32[32,1,2048]{2,1,0:T(1,128)}), f32[32,1,2048]{2,1,0:T(1,128)S(1)}, u32[]{:S(2)}, u32[]{:S(2)}) async-start(f32[32,1,2048]{2,1,0:T(1,128)} %broadcast_in_dim.49), calls=%async_computation.4 | async-start | bytes 524288 | tf_op jit(solution)/shard_map/all_to_all | solution.py:99
  135.6 15.2 %all-to-all-start.5 = ((bf16[4,256,172]{1,2,0:T(8,128)(2,1)}), bf16[4,256,172]{1,2,0:T(8,128)(2,1)S(1)}, u32[]{:S(2)}, u32[]{:S(2)}) async-start(bf16[4,256,172]{1,2,0:T(8,128)(2,1)} %copy.41), calls=%async_computation.5 | async-start | bytes 720896 | tf_op jit(solution)/shard_map/all_to_all | solution.py:217
  139.1 7.4 %copy-start.3 = (bf16[2048,512]{1,0:T(8,128)(2,1)S(1)}, bf16[2048,512]{1,0:T(8,128)(2,1)}, u32[]{:S(2)}) copy-start(bf16[2048,512]{1,0:T(8,128)(2,1)} %pick_rows.1) | copy-start | bytes 6291460
  152.2 20.3 %all-to-all-start.6 = ((bf16[8,72,1024]{2,1,0:T(8,128)(2,1)}), bf16[8,72,1024]{2,1,0:T(8,128)(2,1)S(1)}, u32[]{:S(2)}, u32[]{:S(2)}) async-start(bf16[8,72,1024]{2,1,0:T(8,128)(2,1)} %maximum_maximum_fusion), calls=%async_computation.6 | async-start | bytes 2359296 | tf_op jit(solution)/shard_map/all_to_all | solution.py:230
  172.7 8.0 %collective-permute-start.3 = (f32[64,256]{1,0:T(8,128)S(1)}, f32[64,256]{1,0:T(8,128)S(1)}, u32[]{:S(2)}, u32[]{:S(2)}) collective-permute-start(f32[64,256]{1,0:T(8,128)S(1)} %get-tuple-element.46), channel_id=1, source_target_pairs={{0,1},{1,2},{2,3},{3,0},{4,5},{5,6},{6,7},{7,4},{8,9},{9,10},{10,1... | collective-permute-start | bytes 196616 | tf_op jit(solution)/shard_map/ppermute | solution.py:238
  172.8 8.0 %collective-permute-start.5 = (f32[64,256]{1,0:T(8,128)S(1)}, f32[64,256]{1,0:T(8,128)S(1)}, u32[]{:S(2)}, u32[]{:S(2)}) collective-permute-start(f32[64,256]{1,0:T(8,128)S(1)} %get-tuple-element.47), channel_id=1, source_target_pairs={{0,3},{1,0},{2,1},{3,2},{4,7},{5,4},{6,5},{7,6},{8,11},{9,8},{10,9... | collective-permute-start | bytes 196616 | tf_op jit(solution)/shard_map/ppermute | solution.py:238
  176.6 5.2 %collective-permute-start.4 = (f32[64,256]{1,0:T(8,128)S(1)}, f32[64,256]{1,0:T(8,128)S(1)}, u32[]{:S(2)}, u32[]{:S(2)}) collective-permute-start(f32[64,256]{1,0:T(8,128)S(1)} %get-tuple-element.48), channel_id=1, source_target_pairs={{0,2},{1,3},{2,0},{3,1},{4,6},{5,7},{6,4},{7,5},{8,10},{9,11},{10,... | collective-permute-start | bytes 196616 | tf_op jit(solution)/shard_map/ppermute | solution.py:238
  177.4 10.3 %all-to-all-start.7 = ((f32[8,32,172]{2,1,0:T(8,128)}), f32[8,32,172]{2,1,0:T(8,128)S(1)}, u32[]{:S(2)}, u32[]{:S(2)}) async-start(f32[8,32,172]{2,1,0:T(8,128)} %broadcast_in_dim.50), calls=%async_computation.7 | async-start | bytes 524288 | tf_op jit(solution)/shard_map/all_to_all | solution.py:99
